TPU v7x, 32 devices: a whole 2x2x4 slice. The times are simulated.
32 devices in a mesh: groups: 2 (over x), mix: 16 (over z, y, core).
Axes of the slice: x: 2, y: 2, z: 4, core: 2. Of those that a mesh axis runs over, the one named last changes fastest.
Arguments:
- recording: bfloat16 [8, 16384, 768], P('groups', 'mix'), parts along dimension 0, may hold values from -6 to 6
- mix_gain: float32 [1, 768], replicated, may hold values from 0.25 to 1.75
- block_weights: bfloat16 [1, 4, 128, 2, 128, 128], P(None, None, 'mix'), may hold values from -0.375 to 0.375
- section_perm: int32 [1, 4, 128], replicated, may hold values from 0 to 127, each once within a row
- block_mask: int32 [1, 4, 128], P(None, None, 'mix'), may hold values 0 or 1
- ffn_gain: float32 [1, 768], replicated, may hold values from 0.25 to 1.75
- ffn_in: bfloat16 [1, 2, 768, 2048], P(None, None, None, 'mix'), may hold values from -0.21875 to 0.21875
- ffn_out: bfloat16 [1, 768, 2048], P(None, None, 'mix'), may hold values from -0.125 to 0.125
Outputs:
- encoded: bfloat16 [8, 16384, 768], P('groups', 'mix'), parts along dimension 0
There are 2 independent parts, one for each index of `groups`. A program takes and returns all parts, laid end to end along the dimension named above; an argument that names none is the same for every part. Nothing has to cross between parts.
Inputs may be any that keep to these rules, and one draw needn't show every extreme that they name: Each row section_perm[l, s] holds every number of 0 to 127 once.
All inputs are finite; a program needn't handle non-finite values. No bound on the sum of `block_mask` on one device may be relied on, other than what follows from the above.
Results may differ from a plain program's by a relative error of at most 0.013.
Values may be sent and summed in bfloat16 or wider, within the bound.
A program may use at most 192 MiB of HBM per device.

v0:
```python
import jax
import jax.numpy as jnp
from jax import lax
from jax.sharding import PartitionSpec as P

epsilon = 1e-05


def partner(value, axis, distance):
    mask = 2**distance
    pairs = [(source, source ^ mask) for source in range(lax.axis_size(axis))]
    return lax.ppermute(value, axis, pairs)


def rms_scale(values, gain):
    values = values.astype(jnp.float32)
    mean_sq = jnp.mean(values * values, axis=-1, keepdims=True)
    return values * lax.rsqrt(mean_sq + epsilon) * gain


def on_device(
    recording, mix_gain, block_weights, section_perm, block_mask, ffn_gain, ffn_in, ffn_out
):
    time_steps, local_ch, model_width = recording.shape
    block_size = block_weights.shape[-1]
    per_device = local_ch // block_size
    section_count = block_weights.shape[1]
    total_blocks = lax.axis_size("mix") * per_device
    total_bits = total_blocks.bit_length() - 1
    low_bits = per_device.bit_length() - 1
    row_count = time_steps * local_ch
    current = recording
    normed = rms_scale(current, mix_gain[0]).astype(jnp.bfloat16)
    blocks = normed.reshape(time_steps, per_device, block_size, model_width)
    for section_idx in range(section_count):
        inverse = jnp.argsort(section_perm[0, section_idx])
        weights = jnp.take(block_weights[0, section_idx], inverse, axis=-1)
        own_term = jnp.einsum(
            "joi,tjid->tjod", weights[:, 0], blocks, preferred_element_type=jnp.float32
        )
        far_blocks = partner(blocks, "mix", total_bits - 1 - section_idx - low_bits)
        far_term = jnp.einsum(
            "joi,tjid->tjod", weights[:, 1], far_blocks, preferred_element_type=jnp.float32
        )
        gate_far = block_mask[0, section_idx].astype(jnp.float32)[None, :, None, None]
        blocks = (own_term + gate_far * far_term).astype(jnp.bfloat16)
    mixed_blocks = blocks.reshape(time_steps, local_ch, model_width)
    mixed = (current.astype(jnp.float32) + mixed_blocks.astype(jnp.float32)).astype(jnp.bfloat16)
    mixed_rows = mixed.reshape(row_count, model_width)
    ffn_normed = rms_scale(mixed_rows, ffn_gain[0]).astype(jnp.bfloat16)
    in_piece = lax.all_gather(ffn_in[0], "mix", axis=2, tiled=True)
    gate_proj = jnp.dot(ffn_normed, in_piece[0], preferred_element_type=jnp.float32)
    up_proj = jnp.dot(ffn_normed, in_piece[1], preferred_element_type=jnp.float32)
    hidden_all = (jax.nn.silu(gate_proj) * up_proj).astype(jnp.bfloat16)
    update = lax.dot_general(
        hidden_all,
        lax.all_gather(ffn_out[0], "mix", axis=1, tiled=True),
        (((1,), (1,)), ((), ())),
        preferred_element_type=jnp.float32,
    )
    current = (
        (mixed_rows.astype(jnp.float32) + update)
        .astype(jnp.bfloat16)
        .reshape(time_steps, local_ch, model_width)
    )
    return current


def solution(mesh):
    in_specs = (
        P("groups", "mix", None),
        P(),
        P(None, None, "mix", None, None, None),
        P(),
        P(None, None, "mix"),
        P(),
        P(None, None, None, "mix"),
        P(None, None, "mix"),
    )
    out_specs = P("groups", "mix", None)
    return jax.shard_map(
        on_device, mesh=mesh, in_specs=in_specs, out_specs=out_specs, check_vma=False
    )
```

profile of v0, /device:TPU:19, one launch (start us, length us, event | category | flops | bytes accessed | tf_op | source)
XLA Modules:
  0.0 749.6 jit_solution(10286008892907949539)
XLA Ops:
  6.5 0.0 copy-start.3
  6.5 0.0 all-gather.5.cloned.1.call-start
  6.5 4.1 fusion.2
  10.7 0.0 copy-done.3
  10.7 7.2 fusion.4
  17.9 0.0 copy-start.1
  17.9 0.0 copy-start.5
  17.9 8.8 %copy.14 = bf16[4,8,128,768]{2,3,0,1:T(8,128)(2,1)} copy(bf16[4,8,128,768]{3,2,1,0:T(8,128)(2,1)} %bitcast.116) | data formatting | bytes 12582912 | tf_op jit(solution)/shard_map/reshape | solution.py:34
  26.7 0.0 copy-start.6
  26.7 0.1 collective-permute-start
  26.8 0.0 copy-done.1
  26.8 1.2 fusion.19
  27.9 1.3 copy.36
  29.3 0.0 copy-done.5
  29.3 2.5 sort.59
  31.9 0.8 gather_fusion
  32.6 0.5 copy.12
  33.1 0.0 copy-done.6
  33.1 0.1 select_bitcast_fusion.3
  33.2 9.2 %fusion.16 = f32[8,4,768,128]{3,2,1,0:T(8,128)} fusion(bf16[4,8,128,768]{2,3,0,1:T(8,128)(2,1)} %copy.14, bf16[8,2,128,128]{3,2,0,1:T(8,128)(2,1)S(1)} %select_bitcast_fusion.3), kind=kOutput, calls=%fused_computation.46 | convolution fusion | flops 805306368 | bytes 19136512 | tf_op jit(solution)/shard_map/joi,tjid->tjod/dot_general | solution.py:38
  42.3 253.8 %collective-permute-done = bf16[4,8,128,768]{2,3,0,1:T(8,128)(2,1)} collective-permute-done((bf16[4,8,128,768]{2,3,0,1:T(8,128)(2,1)}, bf16[4,8,128,768]{2,3,0,1:T(8,128)(2,1)}, u32[]{:S(2)}, u32[]{:S(2)}) %collective-permute-start) | collective-permute-done | bytes 6291488 | tf_op jit(solution)/shard_map/ppermute | solution.py:12
  296.1 0.0 copy-start.2
  296.1 11.0 %fusion.7 = bf16[4,8,128,768]{2,3,0,1:T(8,128)(2,1)} fusion(f32[8,4,768,128]{3,2,1,0:T(8,128)} %fusion.16, f32[8]{0:T(128)S(1)} %get-tuple-element.22, bf16[4,8,128,768]{2,3,0,1:T(8,128)(2,1)} %collective-permute-done, bf16[8,2,128,128]{3,2,0,1:T(8,128)(2,1)S(1)} %select_bitcast_fusion.3), kind=kOutput, calls=%fused_computation.23 | convolution fusion | flops 814743552 | bytes 25428480 | tf_op jit(solution)/shard_map/joi,tjid->tjod/dot_general | solution.py:42
  307.1 5.3 collective-permute-start.1
  312.3 0.0 copy-done.2
  312.3 0.3 copy.37
  312.7 2.6 sort.60
  315.3 0.8 gather_fusion.1
  316.0 0.5 copy.16
  316.5 0.1 select_bitcast_fusion.2
  316.6 9.2 %fusion.15 = f32[8,4,768,128]{3,2,1,0:T(8,128)} fusion(bf16[4,8,128,768]{2,3,0,1:T(8,128)(2,1)} %fusion.7, bf16[8,2,128,128]{3,2,0,1:T(8,128)(2,1)S(1)} %select_bitcast_fusion.2), kind=kOutput, calls=%fused_computation.43 | convolution fusion | flops 805306368 | bytes 19136512 | tf_op jit(solution)/shard_map/joi,tjid->tjod/dot_general | solution.py:38
  325.7 122.4 %collective-permute-done.1 = bf16[4,8,128,768]{2,3,0,1:T(8,128)(2,1)} collective-permute-done((bf16[4,8,128,768]{2,3,0,1:T(8,128)(2,1)}, bf16[4,8,128,768]{2,3,0,1:T(8,128)(2,1)}, u32[]{:S(2)}, u32[]{:S(2)}) %collective-permute-start.1) | collective-permute-done | bytes 6291488 | tf_op jit(solution)/shard_map/ppermute | solution.py:12
  448.1 10.9 %fusion.8 = bf16[4,8,128,768]{2,3,0,1:T(8,128)(2,1)} fusion(f32[8,4,768,128]{3,2,1,0:T(8,128)} %fusion.15, f32[8]{0:T(128)S(1)} %get-tuple-element.21, bf16[4,8,128,768]{2,3,0,1:T(8,128)(2,1)} %collective-permute-done.1, bf16[8,2,128,128]{3,2,0,1:T(8,128)(2,1)S(1)} %select_bitcast_fusion.2), kind=kOutput, calls=%fused_computation.24 | convolution fusion | flops 814743552 | bytes 25428480 | tf_op jit(solution)/shard_map/joi,tjid->tjod/dot_general | solution.py:42
  459.0 1.2 collective-permute-start.2
  460.2 0.0 all-gather.5.cloned.1.call-update
  460.3 0.2 all-gather.7.cloned.1.call-start
  460.5 0.3 copy.38
  460.8 2.6 sort.61
  463.4 0.8 gather_fusion.2
  464.2 0.5 copy.18
  464.7 0.1 select_bitcast_fusion.1
  464.7 9.2 %fusion.14 = f32[8,4,768,128]{3,2,1,0:T(8,128)} fusion(bf16[4,8,128,768]{2,3,0,1:T(8,128)(2,1)} %fusion.8, bf16[8,2,128,128]{3,2,0,1:T(8,128)(2,1)S(1)} %select_bitcast_fusion.1), kind=kOutput, calls=%fused_computation.40 | convolution fusion | flops 805306368 | bytes 19136512 | tf_op jit(solution)/shard_map/joi,tjid->tjod/dot_general | solution.py:38
  473.9 142.5 %collective-permute-done.2 = bf16[4,8,128,768]{2,3,0,1:T(8,128)(2,1)} collective-permute-done((bf16[4,8,128,768]{2,3,0,1:T(8,128)(2,1)}, bf16[4,8,128,768]{2,3,0,1:T(8,128)(2,1)}, u32[]{:S(2)}, u32[]{:S(2)}) %collective-permute-start.2) | collective-permute-done | bytes 6291488 | tf_op jit(solution)/shard_map/ppermute | solution.py:12
  616.4 0.0 copy-start.4
  616.4 10.9 %fusion.9 = bf16[4,8,128,768]{2,3,0,1:T(8,128)(2,1)} fusion(f32[8,4,768,128]{3,2,1,0:T(8,128)} %fusion.14, f32[8]{0:T(128)S(1)} %get-tuple-element.23, bf16[4,8,128,768]{2,3,0,1:T(8,128)(2,1)} %collective-permute-done.2, bf16[8,2,128,128]{3,2,0,1:T(8,128)(2,1)S(1)} %select_bitcast_fusion.1), kind=kOutput, calls=%fused_computation.25 | convolution fusion | flops 814743552 | bytes 25428480 | tf_op jit(solution)/shard_map/joi,tjid->tjod/dot_general | solution.py:42
  627.3 1.9 collective-permute-start.3
  629.2 0.0 all-gather.7.cloned.1.call-update
  629.2 0.0 copy-done.4
  629.3 0.3 copy.39
  629.6 2.6 sort.62
  632.2 0.8 gather_fusion.3
  633.0 0.5 copy.20
  633.5 0.1 select_bitcast_fusion
  633.5 9.1 %fusion.13 = f32[8,4,768,128]{2,3,1,0:T(8,128)} fusion(bf16[4,8,128,768]{2,3,0,1:T(8,128)(2,1)} %fusion.9, bf16[8,2,128,128]{3,2,0,1:T(8,128)(2,1)S(1)} %select_bitcast_fusion), kind=kOutput, calls=%fused_computation.37 | convolution fusion | flops 805306368 | bytes 19136512 | tf_op jit(solution)/shard_map/joi,tjid->tjod/dot_general | solution.py:38
  642.6 0.0 collective-permute-done.3
  642.6 12.8 %convert_bitcast_fusion = f32[4,8,128,768]{3,2,0,1:T(8,128)} fusion(f32[8,4,768,128]{2,3,1,0:T(8,128)} %fusion.13, f32[8]{0:T(128)S(1)} %get-tuple-element.20, bf16[4,8,128,768]{2,3,0,1:T(8,128)(2,1)} %collective-permute-done.3, bf16[8,2,128,128]{3,2,0,1:T(8,128)(2,1)S(1)} %select_bitcast_fusion), kind=kOutput, calls=%fused_computation.16 | convolution fusion | flops 817889280 | bytes 31719936 | tf_op jit(solution)/shard_map/joi,tjid->tjod/dot_general | solution.py:42
  655.4 10.9 %copy.23 = f32[4,8,128,768]{3,2,1,0:T(8,128)} copy(f32[4,8,128,768]{3,2,0,1:T(8,128)} %convert_bitcast_fusion) | data formatting | bytes 25165824 | tf_op jit(solution)/shard_map/convert_element_type | solution.py:48
  666.3 7.8 %multiply_reduce_fusion = (f32[4,1024]{1,0:T(4,128)S(1)}, f32[4,1024,768]{2,1,0:T(8,128)S(1)}) fusion(f32[4,8,128,768]{3,2,1,0:T(8,128)} %copy.23, bf16[4,1024,768]{2,1,0:T(8,128)(2,1)} %param.10), kind=kLoop, calls=%fused_computation.18 | loop fusion | flops 18870272 | bytes 31473664 | tf_op jit(solution)/shard_map/reduce_sum | solution.py:17
  674.1 0.0 copy-start
  674.1 4.4 copy-done
  678.6 3.6 multiply_convert_fusion.1
  682.2 0.0 all-gather.5.cloned.1.call-done
  682.2 22.4 %fusion.11 = f32[4096,2048]{1,0:T(8,128)} fusion(bf16[4096,768]{1,0:T(8,128)(2,1)} %bitcast.117, bf16[1,2,768,2048]{3,2,1,0:T(8,128)(2,1)} %all-gather.5.cloned.1.call-done), kind=kOutput, calls=%fused_computation.29 | convolution fusion | flops 12884901888 | bytes 42991616 | tf_op jit(solution)/shard_map/dot_general | solution.py:52
  704.6 37.7 %fusion.6 = bf16[4096,768]{1,0:T(8,128)(2,1)} fusion(f32[4,1024,768]{2,1,0:T(8,128)} %copy-done, f32[4096,2048]{1,0:T(8,128)} %fusion.11, bf16[4096,768]{1,0:T(8,128)(2,1)} %bitcast.118, bf16[1,2,768,2048]{3,2,1,0:T(8,128)(2,1)} %all-gather.5.cloned.1.call-done, bf16[1,768,2048]{2,1,0:T(8,128)(2,1)} %all-gather.7.cloned.1.call-done), kind=kOutput, calls=%fused_computation.15 | convolution fusion | flops 25826426880 | bytes 65011712 | tf_op jit(solution)/shard_map/dot_general | solution.py:55
  (23 shorter events, 0.2 us)
Async XLA Ops:
  6.5 4.1 copy-start.3
  6.5 675.6 %all-gather.5.cloned.1.call-start = ((), (), s32[]{:S(2)}) async-start(), calls=%async_computation | async-start | bytes 6684672 | tf_op jit(solution)/shard_map/all_gather | solution.py:51
  17.9 8.9 %copy-start.1 = (bf16[1,4,8,2,128,128]{5,4,3,2,1,0:T(8,128)(2,1)S(1)}, bf16[1,4,8,2,128,128]{5,4,3,2,1,0:T(8,128)(2,1)}, u32[]{:S(2)}) copy-start(bf16[1,4,8,2,128,128]{5,4,3,2,1,0:T(8,128)(2,1)} %param.12) | copy-start | bytes 6291460
  17.9 11.4 %copy-start.5 = (s32[1,4,128]{2,1,0:T(4,128)S(1)}, s32[1,4,128]{2,1,0:T(4,128)}, u32[]{:S(2)}) copy-start(s32[1,4,128]{2,1,0:T(4,128)} %param.13) | copy-start | bytes 6148
  26.7 6.4 copy-start.6
  26.7 269.4 %collective-permute-start = (bf16[4,8,128,768]{2,3,0,1:T(8,128)(2,1)}, bf16[4,8,128,768]{2,3,0,1:T(8,128)(2,1)}, u32[]{:S(2)}, u32[]{:S(2)}) collective-permute-start(bf16[4,8,128,768]{2,3,0,1:T(8,128)(2,1)} %copy.14), channel_id=1, source_target_pairs={{0,8},{1,9},{2,10},{3,11},{4,12},{5,13},{6,14},{7,15},{8,0},{9,1},... | collective-permute-start | bytes 18874376 | tf_op jit(solution)/shard_map/ppermute | solution.py:12
  296.1 16.2 %copy-start.2 = (bf16[1,1,8,2,128,128]{5,4,3,2,1,0:T(8,128)(2,1)S(1)}, bf16[1,1,8,2,128,128]{5,4,3,2,1,0:T(8,128)(2,1)}, u32[]{:S(2)}) copy-start(bf16[1,1,8,2,128,128]{5,4,3,2,1,0:T(8,128)(2,1)} %get-tuple-element.18) | copy-start | bytes 1572868
  307.1 141.0 %collective-permute-start.1 = (bf16[4,8,128,768]{2,3,0,1:T(8,128)(2,1)}, bf16[4,8,128,768]{2,3,0,1:T(8,128)(2,1)}, u32[]{:S(2)}, u32[]{:S(2)}) collective-permute-start(bf16[4,8,128,768]{2,3,0,1:T(8,128)(2,1)} %fusion.7), channel_id=1, source_target_pairs={{0,4},{1,5},{2,6},{3,7},{4,0},{5,1},{6,2},{7,3},{8,12},{9,13},{10,... | collective-permute-start | bytes 18874376 | tf_op jit(solution)/shard_map/ppermute | solution.py:12
  459.0 157.4 %collective-permute-start.2 = (bf16[4,8,128,768]{2,3,0,1:T(8,128)(2,1)}, bf16[4,8,128,768]{2,3,0,1:T(8,128)(2,1)}, u32[]{:S(2)}, u32[]{:S(2)}) collective-permute-start(bf16[4,8,128,768]{2,3,0,1:T(8,128)(2,1)} %fusion.8), channel_id=1, source_target_pairs={{0,2},{1,3},{2,0},{3,1},{4,6},{5,7},{6,4},{7,5},{8,10},{9,11},{10,... | collective-permute-start | bytes 18874376 | tf_op jit(solution)/shard_map/ppermute | solution.py:12
  460.3 244.3 %all-gather.7.cloned.1.call-start = ((), (), s32[]{:S(2)}) async-start(), calls=%async_computation.1 | async-start | bytes 3342336 | tf_op jit(solution)/shard_map/all_gather | solution.py:57
  616.4 12.9 %copy-start.4 = (f32[1,768]{1,0:T(1,128)S(1)}, f32[1,768]{1,0:T(1,128)}, u32[]{:S(2)}) copy-start(f32[1,768]{1,0:T(1,128)} %param.15) | copy-start | bytes 9220
  627.3 15.3 %collective-permute-start.3 = (bf16[4,8,128,768]{2,3,0,1:T(8,128)(2,1)}, bf16[4,8,128,768]{2,3,0,1:T(8,128)(2,1)}, u32[]{:S(2)}, u32[]{:S(2)}) collective-permute-start(bf16[4,8,128,768]{2,3,0,1:T(8,128)(2,1)} %fusion.9), channel_id=1, source_target_pairs={{0,1},{1,0},{2,3},{3,2},{4,5},{5,4},{6,7},{7,6},{8,9},{9,8},{10,11... | collective-permute-start | bytes 18874376 | tf_op jit(solution)/shard_map/ppermute | solution.py:12
  674.1 4.5 copy-start
Sparse Core Ops, SparseCore 0:
  460.4 87.8 all-gather.4
  629.4 47.1 all-gather.6
where the time goes:
time: 759 us; the launch traced here: 750 us
  waiting for transfers between devices  519 us (68%)
  matrix products  142 us (19%)
  other arithmetic  33.4 us (4%)
  local copies, waits for them, and re-layouts  32.6 us (4%)
  between operations  14.1 us (2%)
  starting transfers between devices  8.71 us (1%)
    ppermute x4, waiting for transfers between devices, partner(): return lax.ppermute(value, axis, pairs)  519 us
    dot_general x4, matrix products, on_device(): jnp.einsum('joi,tjid->tjod', weights[:, 1], far_blocks, preferred_element...  45.6 us
    dot_general x1, matrix products, on_device(): lax.dot_general(hidden_all, lax.all_gather(ffn_out[0], 'mix', axis=1, til...  37.7 us
    dot_general x4, matrix products, on_device(): jnp.einsum('joi,tjid->tjod', weights[:, 0], blocks, preferred_element_typ...  36.5 us
    dot_general x1, matrix products, on_device(): jnp.dot(ffn_normed, in_piece[0], preferred_element_type=jnp.float32)  22.4 us
  transfers between devices with their start and end apart: 6, of which 3 were waited for; matrix products, arithmetic and copies ran while one was open for 17% of the time, Pallas kernels for 0%

commit v1 on v0

v1 whole, which is shorter than its diff:
```python
import functools

import jax
import jax.numpy as jnp
from jax import lax
from jax.experimental import pallas as pl
from jax.experimental.pallas import tpu as pltpu
from jax.sharding import PartitionSpec as P

epsilon = 1e-05
WINDOW = 4
RING = 4
FTILE = 512


def rms_scale(values, gain):
    values = values.astype(jnp.float32)
    mean_sq = jnp.mean(values * values, axis=-1, keepdims=True)
    return values * lax.rsqrt(mean_sq + epsilon) * gain


def mixing_kernel(
    dims,
    x_ref,
    gain1_ref,
    bw_ref,
    perm_ref,
    mask_ref,
    gain2_ref,
    wl_ref,
    out_ref,
    own0,
    ring,
    far,
    wc,
    wf,
    hn,
    acc,
    send_sem,
    recv_sem,
    ag_send,
    ag_recv,
    local_sem,
    out_sem,
):
    n_dev, sections, nb, batch, first_bit = dims
    chunks, blk, width = x_ref.shape
    hidden_units = wf.shape[1]
    shard = wl_ref.shape[1]
    n_batches = chunks // batch
    bits = n_dev.bit_length() - 1
    last = sections - 1
    me = lax.axis_index("mix")
    partners = [me + (1 << b) * (1 - 2 * ((me // (1 << b)) % 2)) for b in range(bits)]

    local = pltpu.make_async_copy(wl_ref, wf.at[:, pl.ds(0, shard), :], local_sem)
    local.start()

    barrier = pltpu.get_barrier_semaphore()
    for b in range(bits):
        pl.semaphore_signal(
            barrier, inc=1, device_id={"mix": partners[b]}, device_id_type=pl.DeviceIdType.MESH
        )
    pl.semaphore_wait(barrier, bits)

    def own_at(s, k):
        return own0.at[k] if s == 0 else ring.at[s - 1, k % RING]

    def exchange(s, k):
        return pltpu.make_async_remote_copy(
            src_ref=own_at(s, k),
            dst_ref=far.at[s, k],
            send_sem=send_sem.at[s, k],
            recv_sem=recv_sem.at[s, k],
            device_id={"mix": partners[first_bit - s]},
            device_id_type=pl.DeviceIdType.MESH,
        )

    def gather_step(g):
        count = shard << g
        return pltpu.make_async_remote_copy(
            src_ref=wf.at[:, pl.ds(0, count), :],
            dst_ref=wf.at[:, pl.ds(count, count), :],
            send_sem=ag_send.at[g],
            recv_sem=ag_recv.at[g],
            device_id={"mix": partners[bits - 1 - g]},
            device_id_type=pl.DeviceIdType.MESH,
        )

    def norm_and_send(k):
        own0[k] = rms_scale(x_ref[k], gain1_ref[...]).astype(jnp.bfloat16)
        exchange(0, k).start()

    def first(k, carry):
        norm_and_send(k)
        return carry

    window = min(WINDOW, chunks)
    lax.fori_loop(0, window, first, 0)
    if bits:
        local.wait()
        gather_step(0).start()

    def fold(q, carry):
        s = q // nb
        where_to = lax.broadcasted_iota(jnp.int32, (blk, blk), 1)
        hot = (perm_ref[s] == where_to).astype(jnp.float32).astype(jnp.bfloat16)
        keep = mask_ref[q].astype(jnp.float32)
        wc[q, :, :blk] = jnp.dot(
            bw_ref[q, 0], hot, preferred_element_type=jnp.float32
        ).astype(jnp.bfloat16)
        wc[q, :, blk:] = (
            keep * jnp.dot(bw_ref[q, 1], hot, preferred_element_type=jnp.float32)
        ).astype(jnp.bfloat16)
        return carry

    lax.fori_loop(0, sections * nb, fold, 0)

    def section(s, k):
        both = jnp.concatenate([own_at(s, k)[...], far[s, k]], axis=0)
        return jnp.dot(
            wc[s * nb + k % nb], both, preferred_element_type=jnp.float32
        ).astype(jnp.bfloat16)

    def ffn(b, carry):
        rows = batch * blk
        base = pl.multiple_of(b * batch, batch)
        mixed = own0[pl.ds(base, batch)].reshape(rows, width)
        hn[...] = rms_scale(mixed, gain2_ref[...]).astype(jnp.bfloat16)
        acc[...] = mixed.astype(jnp.float32)

        def tile(f, inner):
            at = pl.ds(pl.multiple_of(f * FTILE, FTILE), FTILE)
            nt = (((1,), (1,)), ((), ()))
            gate = lax.dot_general(hn[...], wf[0, at, :], nt, preferred_element_type=jnp.float32)
            up = lax.dot_general(hn[...], wf[1, at, :], nt, preferred_element_type=jnp.float32)
            hidden = (gate / (1.0 + jnp.exp(-gate)) * up).astype(jnp.bfloat16)
            acc[...] += jnp.dot(hidden, wf[2, at, :], preferred_element_type=jnp.float32)
            return inner

        lax.fori_loop(0, hidden_units // FTILE, tile, 0)
        own0[pl.ds(base, batch)] = acc[...].astype(jnp.bfloat16).reshape(batch, blk, width)
        pltpu.make_async_copy(
            own0.at[pl.ds(base, batch)], out_ref.at[pl.ds(base, batch)], out_sem.at[b]
        ).start()
        return carry

    ffn_from = chunks // 2 + 1
    gather_at = [1 + g * (ffn_from - 1) // max(bits, 1) for g in range(bits)]

    def ready(i):
        done = jnp.clip((i - last + 1) // batch, 0, n_batches)
        return jnp.where(i >= ffn_from, done, 0)

    def step(i, carry):
        for g in range(1, bits):

            @pl.when(i == gather_at[g])
            def _(g=g):
                gather_step(g - 1).wait_recv()
                gather_step(g).start()

        @pl.when(i + window < chunks)
        def _():
            norm_and_send(i + window)

        for s in range(sections):
            k = i - s

            @pl.when(jnp.logical_and(k >= 0, k < chunks))
            def _(s=s, k=k):
                exchange(s, k).wait_recv()
                result = section(s, k)
                if s < last:

                    @pl.when(k >= RING)
                    def _():
                        exchange(s + 1, k - RING).wait_send()

                    own_at(s + 1, k)[...] = result
                    exchange(s + 1, k).start()
                else:
                    exchange(0, k).wait_send()
                    own0[k] = (
                        x_ref[k].astype(jnp.float32) + result.astype(jnp.float32)
                    ).astype(jnp.bfloat16)

        if bits:

            @pl.when(i == ffn_from)
            def _():
                gather_step(bits - 1).wait_recv()

        lax.fori_loop(ready(i - 1), ready(i), ffn, 0)
        return carry

    lax.fori_loop(0, chunks + last, step, 0)

    for s in range(1, sections):
        for k in range(max(chunks - RING, 0), chunks):
            exchange(s, k).wait_send()
    for g in range(bits):
        gather_step(g).wait_send()
    for b in range(n_batches):
        at = pl.ds(b * batch, batch)
        pltpu.make_async_copy(own0.at[at], out_ref.at[at], out_sem.at[b]).wait()


def on_device(
    recording, mix_gain, block_weights, section_perm, block_mask, ffn_gain, ffn_in, ffn_out
):
    time_steps, local_ch, width = recording.shape
    sections, nb, _, blk, _ = block_weights.shape[1:]
    n_dev = lax.axis_size("mix")
    chunks = time_steps * nb
    batch = 4
    while chunks % batch:
        batch //= 2
    bits = n_dev.bit_length() - 1
    total_bits = (n_dev * nb).bit_length() - 1
    first_bit = total_bits - 1 - (nb.bit_length() - 1)
    shard = ffn_in.shape[-1]
    local_weights = jnp.concatenate(
        [jnp.swapaxes(ffn_in[0], 1, 2), jnp.swapaxes(ffn_out, 1, 2)], axis=0
    )
    vmem = pl.BlockSpec(memory_space=pltpu.VMEM)
    anywhere = pl.BlockSpec(memory_space=pl.ANY)
    result = pl.pallas_call(
        functools.partial(mixing_kernel, (n_dev, sections, nb, batch, first_bit)),
        out_shape=jax.ShapeDtypeStruct((chunks, blk, width), jnp.bfloat16),
        in_specs=[vmem, vmem, vmem, vmem, pl.BlockSpec(memory_space=pltpu.SMEM), vmem, anywhere],
        out_specs=anywhere,
        scratch_shapes=[
            pltpu.VMEM((chunks, blk, width), jnp.bfloat16),
            pltpu.VMEM((sections - 1, RING, blk, width), jnp.bfloat16),
            pltpu.VMEM((sections, chunks, blk, width), jnp.bfloat16),
            pltpu.VMEM((sections * nb, blk, 2 * blk), jnp.bfloat16),
            pltpu.VMEM((3, shard * n_dev, width), jnp.bfloat16),
            pltpu.VMEM((batch * blk, width), jnp.bfloat16),
            pltpu.VMEM((batch * blk, width), jnp.float32),
            pltpu.SemaphoreType.DMA((sections, chunks)),
            pltpu.SemaphoreType.DMA((sections, chunks)),
            pltpu.SemaphoreType.DMA((bits,)),
            pltpu.SemaphoreType.DMA((bits,)),
            pltpu.SemaphoreType.DMA,
            pltpu.SemaphoreType.DMA((chunks // batch,)),
        ],
        compiler_params=pltpu.CompilerParams(
            collective_id=0, has_side_effects=True, vmem_limit_bytes=60 * 1024 * 1024
        ),
    )(
        recording.reshape(chunks, blk, width),
        mix_gain,
        block_weights[0].reshape(sections * nb, 2, blk, blk),
        section_perm[0][:, :, None],
        block_mask[0].reshape(sections * nb),
        ffn_gain,
        local_weights,
    )
    return result.reshape(time_steps, local_ch, width)


def solution(mesh):
    in_specs = (
        P("groups", "mix", None),
        P(),
        P(None, None, "mix", None, None, None),
        P(),
        P(None, None, "mix"),
        P(),
        P(None, None, None, "mix"),
        P(None, None, "mix"),
    )
    out_specs = P("groups", "mix", None)
    return jax.shard_map(
        on_device, mesh=mesh, in_specs=in_specs, out_specs=out_specs, check_vma=False
    )
```

time: 759 us -> 441 us (0.58); the launches traced: 750 us -> 440 us
  waiting for transfers between devices: 519 us -> 0 us
  Pallas kernels: 0 us -> 428 us
  matrix products: 142 us -> 0 us
  other arithmetic: 33.4 us -> 0.87 us
  local copies, waits for them, and re-layouts: 32.6 us -> 11 us
  between operations: 14.1 us -> 0.02 us
  starting transfers between devices: 8.71 us -> 0 us
    ppermute x4 -> x0, waiting for transfers between devices: 519 us -> none  [partner(): return lax.ppermute(value, axis, pairs)]
    pallas_call x0 -> x1, Pallas kernels: none -> 428 us  [on_device(): pl.pallas_call(functools.partial(mixing_kernel, (n_dev, sections, nb, bat...]
    dot_general x10 -> x0, matrix products: 142 us -> none  [the longest x4 45.6 us: on_device(): jnp.einsum('joi,tjid->tjod', weights[:, 1], far_blocks, preferred_element...]
    reduce_sum x2 -> x0, other arithmetic: 11.9 us -> none  [rms_scale(): mean_sq = jnp.mean(values * values, axis=-1, keepdims=True)]
    convert_element_type x1 -> x0, local copies, waits for them, and re-layouts: 10.9 us -> none  [on_device(): mixed_blocks.astype(jnp.float32)]
    convert_element_type x3 -> x0, other arithmetic: 10.8 us -> none  [the longest x1 7.16 us: on_device(): normed = rms_scale(current, mix_gain[0]).astype(jnp.bfloat16)]
    sort x4 -> x0, other arithmetic: 10.4 us -> none  [on_device(): inverse = jnp.argsort(section_perm[0, section_idx])]
    reshape x1 -> x0, local copies, waits for them, and re-layouts: 8.85 us -> none  [on_device(): blocks = normed.reshape(time_steps, per_device, block_size, model_width)]
  transfers between devices with their start and end apart: 6 -> 0, of which waited for: 3 -> 0; matrix products, arithmetic and copies ran while one was open for 17% -> 0% of each run, Pallas kernels for 0% -> 0%
where the time goes in v1:
time: 441 us; the launch traced here: 440 us
  Pallas kernels  428 us (97%)
  local copies, waits for them, and re-layouts  11 us (2%)
    pallas_call x1, Pallas kernels, on_device(): pl.pallas_call(functools.partial(mixing_kernel, (n_dev, sections, nb, bat...  428 us

profile of v1, /device:TPU:19, one launch (start us, length us, event | category | flops | bytes accessed | tf_op | source)
XLA Modules:
  0.0 439.6 jit_solution(15892511184043550285)
XLA Ops:
  0.0 1.3 reshape_squeeze.7.mask_ref
  1.3 1.1 copy.12
  2.4 1.5 copy.13.perm_ref
  3.9 1.2 copy.11
  5.1 0.9 pad_maximum_fusion.wl_ref
  5.9 427.8 %shard_map.82 = bf16[32,128,768]{2,1,0:T(8,128)(2,1)} custom-call(bf16[32,128,768]{2,1,0:T(8,128)(2,1)} %bitcast.9, f32[1,768]{1,0:T(1,128)} %gain1_ref.1, bf16[32,2,128,128]{3,2,1,0:T(8,128)(2,1)} %bitcast.10, s32[4,128,1]{2,1,0:T(8,128)} %copy.13.perm_ref, s32[32]{0:T(128)} %reshape_squeeze.7.mask_ref, f32[1,768]{1,0:T(1,128)} %gain2_ref.1, ...), custom_call_target="tpu_custom_call" | custom-call | tf_op jit(solution)/shard_map/pallas_call | solution.py:228
  433.7 5.9 %copy.15 = bf16[4,1024,768]{2,1,0:T(8,128)(2,1)} copy(bf16[4,1024,768]{2,1,0:T(8,128)(2,1)} %bitcast.8) | data formatting | bytes 12582912

commit v2 on v1

--- a/solution.py
+++ b/solution.py
@@ -9,7 +9,8 @@
 
 epsilon = 1e-05
 WINDOW = 4
-RING = 4
+LAG = 4
+RING = 8
 FTILE = 512
 
 
@@ -43,25 +44,35 @@
     local_sem,
     out_sem,
 ):
-    n_dev, sections, nb, batch, first_bit = dims
+    n_dev, sections, nb, batch, first_bit, split = dims
     chunks, blk, width = x_ref.shape
     hidden_units = wf.shape[1]
-    shard = wl_ref.shape[1]
+    shard = wl_ref.shape[1] // split
     n_batches = chunks // batch
     bits = n_dev.bit_length() - 1
     last = sections - 1
     me = lax.axis_index("mix")
     partners = [me + (1 << b) * (1 - 2 * ((me // (1 << b)) % 2)) for b in range(bits)]
 
-    local = pltpu.make_async_copy(wl_ref, wf.at[:, pl.ds(0, shard), :], local_sem)
+    group = lax.axis_index("groups")
+    sibling = group + 1 - 2 * (group % 2)
+    targets = [{"mix": partners[b]} for b in range(bits)]
+    if split == 2:
+        targets = targets + [{"groups": sibling}]
+    piece = pl.ds(pl.multiple_of((group % split) * shard, shard), shard)
+    local = pltpu.make_async_copy(
+        wl_ref.at[:, piece, :], wf.at[:, pl.ds(0, shard), :], local_sem
+    )
     local.start()
+    route = [targets[b] for b in range(bits - 1, 0, -1)] + targets[bits:] + targets[: min(bits, 1)]
+    rounds = len(route)
 
     barrier = pltpu.get_barrier_semaphore()
-    for b in range(bits):
+    for target in targets:
         pl.semaphore_signal(
-            barrier, inc=1, device_id={"mix": partners[b]}, device_id_type=pl.DeviceIdType.MESH
+            barrier, inc=1, device_id=target, device_id_type=pl.DeviceIdType.MESH
         )
-    pl.semaphore_wait(barrier, bits)
+    pl.semaphore_wait(barrier, len(targets))
 
     def own_at(s, k):
         return own0.at[k] if s == 0 else ring.at[s - 1, k % RING]
@@ -83,7 +94,7 @@
             dst_ref=wf.at[:, pl.ds(count, count), :],
             send_sem=ag_send.at[g],
             recv_sem=ag_recv.at[g],
-            device_id={"mix": partners[bits - 1 - g]},
+            device_id=route[g],
             device_id_type=pl.DeviceIdType.MESH,
         )
 
@@ -97,8 +108,8 @@
 
     window = min(WINDOW, chunks)
     lax.fori_loop(0, window, first, 0)
-    if bits:
-        local.wait()
+    local.wait()
+    if rounds:
         gather_step(0).start()
 
     def fold(q, carry):
@@ -146,14 +157,14 @@
         return carry
 
     ffn_from = chunks // 2 + 1
-    gather_at = [1 + g * (ffn_from - 1) // max(bits, 1) for g in range(bits)]
+    gather_at = [1 + g * (ffn_from - 1) // max(rounds, 1) for g in range(rounds)]
 
     def ready(i):
-        done = jnp.clip((i - last + 1) // batch, 0, n_batches)
+        done = jnp.clip((i - last * LAG + 1) // batch, 0, n_batches)
         return jnp.where(i >= ffn_from, done, 0)
 
     def step(i, carry):
-        for g in range(1, bits):
+        for g in range(1, rounds):
 
             @pl.when(i == gather_at[g])
             def _(g=g):
@@ -165,7 +176,7 @@
             norm_and_send(i + window)
 
         for s in range(sections):
-            k = i - s
+            k = i - s * LAG
 
             @pl.when(jnp.logical_and(k >= 0, k < chunks))
             def _(s=s, k=k):
@@ -185,21 +196,21 @@
                         x_ref[k].astype(jnp.float32) + result.astype(jnp.float32)
                     ).astype(jnp.bfloat16)
 
-        if bits:
+        if rounds:
 
             @pl.when(i == ffn_from)
             def _():
-                gather_step(bits - 1).wait_recv()
+                gather_step(rounds - 1).wait_recv()
 
         lax.fori_loop(ready(i - 1), ready(i), ffn, 0)
         return carry
 
-    lax.fori_loop(0, chunks + last, step, 0)
+    lax.fori_loop(0, chunks + last * LAG, step, 0)
 
     for s in range(1, sections):
         for k in range(max(chunks - RING, 0), chunks):
             exchange(s, k).wait_send()
-    for g in range(bits):
+    for g in range(rounds):
         gather_step(g).wait_send()
     for b in range(n_batches):
         at = pl.ds(b * batch, batch)
@@ -220,13 +231,15 @@
     total_bits = (n_dev * nb).bit_length() - 1
     first_bit = total_bits - 1 - (nb.bit_length() - 1)
     shard = ffn_in.shape[-1]
+    split = 2 if lax.axis_size("groups") % 2 == 0 and shard % 32 == 0 else 1
+    rounds = bits + split - 1
     local_weights = jnp.concatenate(
         [jnp.swapaxes(ffn_in[0], 1, 2), jnp.swapaxes(ffn_out, 1, 2)], axis=0
     )
     vmem = pl.BlockSpec(memory_space=pltpu.VMEM)
     anywhere = pl.BlockSpec(memory_space=pl.ANY)
     result = pl.pallas_call(
-        functools.partial(mixing_kernel, (n_dev, sections, nb, batch, first_bit)),
+        functools.partial(mixing_kernel, (n_dev, sections, nb, batch, first_bit, split)),
         out_shape=jax.ShapeDtypeStruct((chunks, blk, width), jnp.bfloat16),
         in_specs=[vmem, vmem, vmem, vmem, pl.BlockSpec(memory_space=pltpu.SMEM), vmem, anywhere],
         out_specs=anywhere,
@@ -240,8 +253,8 @@
             pltpu.VMEM((batch * blk, width), jnp.float32),
             pltpu.SemaphoreType.DMA((sections, chunks)),
             pltpu.SemaphoreType.DMA((sections, chunks)),
-            pltpu.SemaphoreType.DMA((bits,)),
-            pltpu.SemaphoreType.DMA((bits,)),
+            pltpu.SemaphoreType.DMA((rounds,)),
+            pltpu.SemaphoreType.DMA((rounds,)),
             pltpu.SemaphoreType.DMA,
             pltpu.SemaphoreType.DMA((chunks // batch,)),
         ],

time: 441 us -> 351 us (0.80)
  Pallas kernels: 428 us -> 336 us
    pallas_call x1, Pallas kernels: 428 us -> 336 us  [on_device(): pl.pallas_call(functools.partial(mixing_kernel, (n_dev, sections, nb, bat...]
where the time goes in v2:
time: 351 us; the launch traced here: 348 us
  Pallas kernels  336 us (96%)
  local copies, waits for them, and re-layouts  11 us (3%)
    pallas_call x1, Pallas kernels, on_device(): pl.pallas_call(functools.partial(mixing_kernel, (n_dev, sections, nb, bat...  336 us
    unnamed x3, local copies, waits for them, and re-layouts  8.12 us

profile of v2, /device:TPU:19, one launch (start us, length us, event | category | flops | bytes accessed | tf_op | source)
XLA Modules:
  0.0 348.2 jit_solution(17561669610036157397)
XLA Ops:
  0.0 1.3 reshape_squeeze.7.mask_ref
  1.3 1.1 copy.12
  2.4 1.5 copy.13.perm_ref
  3.9 1.2 copy.11
  5.1 0.9 pad_maximum_fusion.wl_ref
  5.9 336.4 %shard_map.82 = bf16[32,128,768]{2,1,0:T(8,128)(2,1)} custom-call(bf16[32,128,768]{2,1,0:T(8,128)(2,1)} %bitcast.9, f32[1,768]{1,0:T(1,128)} %gain1_ref.1, bf16[32,2,128,128]{3,2,1,0:T(8,128)(2,1)} %bitcast.10, s32[4,128,1]{2,1,0:T(8,128)} %copy.13.perm_ref, s32[32]{0:T(128)} %reshape_squeeze.7.mask_ref, f32[1,768]{1,0:T(1,128)} %gain2_ref.1, ...), custom_call_target="tpu_custom_call" | custom-call | tf_op jit(solution)/shard_map/pallas_call | solution.py:241
  342.3 5.9 %copy.15 = bf16[4,1024,768]{2,1,0:T(8,128)(2,1)} copy(bf16[4,1024,768]{2,1,0:T(8,128)(2,1)} %bitcast.8) | data formatting | bytes 12582912

commit v3 on v2

--- a/solution.py
+++ b/solution.py
@@ -9,7 +9,7 @@
 
 epsilon = 1e-05
 WINDOW = 4
-LAG = 4
+OFFSETS = (0, 4, 7, 9)
 RING = 8
 FTILE = 512
 
@@ -156,11 +156,11 @@
         ).start()
         return carry
 
-    ffn_from = chunks // 2 + 1
+    ffn_from = 5 * chunks // 8 + 1
     gather_at = [1 + g * (ffn_from - 1) // max(rounds, 1) for g in range(rounds)]
 
     def ready(i):
-        done = jnp.clip((i - last * LAG + 1) // batch, 0, n_batches)
+        done = jnp.clip((i - OFFSETS[last] + 1) // batch, 0, n_batches)
         return jnp.where(i >= ffn_from, done, 0)
 
     def step(i, carry):
@@ -176,7 +176,7 @@
             norm_and_send(i + window)
 
         for s in range(sections):
-            k = i - s * LAG
+            k = i - OFFSETS[s]
 
             @pl.when(jnp.logical_and(k >= 0, k < chunks))
             def _(s=s, k=k):
@@ -205,7 +205,7 @@
         lax.fori_loop(ready(i - 1), ready(i), ffn, 0)
         return carry
 
-    lax.fori_loop(0, chunks + last * LAG, step, 0)
+    lax.fori_loop(0, chunks + OFFSETS[last], step, 0)
 
     for s in range(1, sections):
         for k in range(max(chunks - RING, 0), chunks):

time: 351 us -> 345 us (0.983)
    pallas_call x1, Pallas kernels: 336 us -> 333 us  [on_device(): pl.pallas_call(functools.partial(mixing_kernel, (n_dev, sections, nb, bat...]
where the time goes in v3:
time: 345 us
  Pallas kernels  333 us (97%)
  local copies, waits for them, and re-layouts  11 us (3%)
    pallas_call x1, Pallas kernels, on_device(): pl.pallas_call(functools.partial(mixing_kernel, (n_dev, sections, nb, bat...  333 us
    unnamed x3, local copies, waits for them, and re-layouts  8.12 us

profile of v3, /device:TPU:19, one launch (start us, length us, event | category | flops | bytes accessed | tf_op | source)
XLA Modules:
  0.0 344.5 jit_solution(6931612443859693072)
XLA Ops:
  0.0 1.3 reshape_squeeze.7.mask_ref
  1.3 1.1 copy.12
  2.4 1.5 copy.13.perm_ref
  3.9 1.2 copy.11
  5.1 0.9 pad_maximum_fusion.wl_ref
  5.9 332.7 %shard_map.82 = bf16[32,128,768]{2,1,0:T(8,128)(2,1)} custom-call(bf16[32,128,768]{2,1,0:T(8,128)(2,1)} %bitcast.9, f32[1,768]{1,0:T(1,128)} %gain1_ref.1, bf16[32,2,128,128]{3,2,1,0:T(8,128)(2,1)} %bitcast.10, s32[4,128,1]{2,1,0:T(8,128)} %copy.13.perm_ref, s32[32]{0:T(128)} %reshape_squeeze.7.mask_ref, f32[1,768]{1,0:T(1,128)} %gain2_ref.1, ...), custom_call_target="tpu_custom_call" | custom-call | tf_op jit(solution)/shard_map/pallas_call | solution.py:241
  338.6 5.9 %copy.15 = bf16[4,1024,768]{2,1,0:T(8,128)(2,1)} copy(bf16[4,1024,768]{2,1,0:T(8,128)(2,1)} %bitcast.8) | data formatting | bytes 12582912
